TPU v7x, 32 devices: a whole 2x2x4 slice. The times are simulated.
32 devices in a mesh: row: 8 (over z, y), col: 4 (over x, core).
Axes of the slice: x: 2, y: 2, z: 4, core: 2. Of those that a mesh axis runs over, the one named last changes fastest.
Arguments:
- start_block: float32 [64, 16, 128], P(('row', 'col')), may hold values from -6 to 6
- blocks: float32 [8, 4, 58, 128, 128], P('row', 'col'), as said below
- slot_row: int32 [8, 4, 58], P('row', 'col'), may hold values from 0 to 7, as said below
- slot_col: int32 [8, 4, 58], P('row', 'col'), may hold values from 0 to 15, as said below
- counts: int32 [8, 4], P('row', 'col'), may hold values from 34 to 58, as said below
Outputs:
- alphas: float32 [2, 16, 16], replicated
- betas: float32 [2, 16, 16], replicated
- next_block: float32 [64, 16, 128], P(('row', 'col'))
Inputs may be any that keep to these rules, and one draw needn't show every extreme that they name: `blocks`: over all cells the live slots list each nonzero block of a symmetric matrix exactly once: block (J, I) is listed exactly when (I, J) is, holding its transpose. Slots at or past a cell's count hold finite values that are no part of H. `counts`: live slots of a cell come first; in every draw some cell has all 58 slots live. `slot_row`: for live slots, the block row within the cell's row group of 8 block rows. `slot_col`: for live slots, the position within the cell's column group of 16 block columns, as in the first step.
All inputs are finite; a program needn't handle non-finite values.
Results may differ from a plain program's by a relative error of at most 0.0003.
Values sent between devices are 32-bit elements; how exact they have to be, the bound alone decides.
A program may use at most 64 MiB of HBM per device.

v0:
```python
import jax
import jax.numpy as jnp
from jax import lax
from jax.sharding import PartitionSpec as P

ITERS = 2
highest = lax.Precision.HIGHEST


def matmul(left, right):
    return jnp.dot(left, right, precision=highest, preferred_element_type=jnp.float32)


def local_gram(left, right):
    return jnp.einsum(
        "bki,bli->kl", left, right, precision=highest, preferred_element_type=jnp.float32
    )


def on_device(start_block, blocks, slot_row, slot_col, counts):
    matrix_tiles = blocks[0, 0]
    rows_local = slot_row[0, 0]
    cols_local = slot_col[0, 0]
    capacity = matrix_tiles.shape[0]
    active = lax.iota(jnp.int32, capacity) < counts[0, 0]
    piece_rows = start_block.shape[0]
    vec_count = start_block.shape[1]
    orbitals = start_block.shape[2]
    row_total = float(piece_rows * lax.axis_size("row") * lax.axis_size("col") * orbitals)
    identity = jnp.eye(vec_count, dtype=jnp.float32)
    start_mean = lax.psum(local_gram(start_block, start_block), ("row", "col")) / row_total
    factor = jnp.linalg.cholesky(start_mean)
    inverse = jax.scipy.linalg.solve_triangular(factor, identity, lower=True)
    vectors = jnp.einsum(
        "kl,bli->bki", inverse, start_block, precision=highest, preferred_element_type=jnp.float32
    )
    previous = jnp.zeros(vectors.shape, jnp.float32)
    beta_prev = jnp.zeros((vec_count, vec_count), jnp.float32)
    alpha_list = []
    beta_list = []
    for iteration in range(ITERS):
        gathered = lax.all_gather(vectors, "row", axis=0, tiled=True)
        operate_product = jnp.einsum(
            "sij,skj->ski",
            matrix_tiles,
            gathered[cols_local],
            precision=highest,
            preferred_element_type=jnp.float32,
        )
        targets = lax.iota(jnp.int32, lax.axis_size("col") * piece_rows)
        selector = ((rows_local[None, :] == targets[:, None]) & active[None, :]).astype(jnp.float32)
        image_block = lax.psum_scatter(
            jnp.einsum(
                "rs,ski->rki",
                selector,
                operate_product,
                precision=highest,
                preferred_element_type=jnp.float32,
            ),
            "col",
            scatter_dimension=0,
            tiled=True,
        )
        stacked = jnp.concatenate([image_block, vectors, previous], axis=1)
        all_means = lax.psum(local_gram(stacked, stacked), ("row", "col")) / row_total
        yy_mean = all_means[:vec_count, :vec_count]
        vy_mean = all_means[vec_count : 2 * vec_count, :vec_count]
        py_mean = all_means[2 * vec_count :, :vec_count]
        vv_mean = all_means[vec_count : 2 * vec_count, vec_count : 2 * vec_count]
        pv_mean = all_means[2 * vec_count :, vec_count : 2 * vec_count]
        pp_mean = all_means[2 * vec_count :, 2 * vec_count :]
        residual = image_block - jnp.einsum(
            "lk,bli->bki", vy_mean, vectors, precision=highest, preferred_element_type=jnp.float32
        )
        residual = residual - jnp.einsum(
            "kl,bli->bki",
            beta_prev,
            previous,
            precision=highest,
            preferred_element_type=jnp.float32,
        )
        gram_mean = yy_mean - matmul(vy_mean.T, vy_mean) - matmul(vy_mean.T, vy_mean)
        gram_mean = gram_mean + matmul(matmul(vy_mean.T, vv_mean), vy_mean)
        gram_mean = gram_mean - matmul(py_mean.T, beta_prev.T) - matmul(beta_prev, py_mean)
        gram_mean = gram_mean + matmul(matmul(vy_mean.T, pv_mean.T), beta_prev.T)
        gram_mean = gram_mean + matmul(matmul(beta_prev, pv_mean), vy_mean)
        gram_mean = gram_mean + matmul(matmul(beta_prev, pp_mean), beta_prev.T)
        factor = jnp.linalg.cholesky(gram_mean)
        beta_block = factor.T
        inverse = jax.scipy.linalg.solve_triangular(factor, identity, lower=True)
        previous = vectors
        vectors = jnp.einsum(
            "kl,bli->bki", inverse, residual, precision=highest, preferred_element_type=jnp.float32
        )
        beta_prev = beta_block
        alpha_list.append(vy_mean)
        beta_list.append(beta_block)
    return (jnp.stack(alpha_list), jnp.stack(beta_list), vectors)


def solution(mesh):
    placed = (
        P(("row", "col"), None, None),
        P("row", "col", None, None, None),
        P("row", "col", None),
        P("row", "col", None),
        P("row", "col"),
    )
    return jax.shard_map(
        on_device,
        mesh=mesh,
        in_specs=placed,
        out_specs=(P(), P(), P(("row", "col"), None, None)),
        check_vma=False,
    )
```

profile of v0, /device:TPU:0, one launch (start us, length us, event | category | flops | bytes accessed | tf_op | source)
XLA Modules:
  0.0 285.7 jit_solution(17474431526224107313)
XLA Ops:
  7.9 0.7 fusion.84
  8.6 0.1 convolution_bitcast_fusion.12
  8.7 42.0 %psum.21 = f32[16,16]{0,1:T(8,128)S(1)} all-reduce(f32[16,16]{0,1:T(8,128)S(1)} %convolution_bitcast_fusion.12), channel_id=1, replica_groups=mesh['row'=8,'col'=4] {'row','col'}, use_global_device_ids=true, to_apply=%region_0.0 | all-reduce | flops 256 | bytes 2048 | tf_op jit(solution)/shard_map/psum | solution.py:31
  50.8 1.5 cholesky.59
  52.3 0.6 compare_reduce_fusion.2
  52.9 0.6 fusion.25
  53.6 1.2 custom-call.7
  54.8 0.2 convolution_bitcast_fusion.11
  55.0 0.1 convolution_bitcast_fusion.8
  55.1 30.6 %all_gather.6 = f32[16,16,128]{2,1,0:T(8,128)S(1)} all-gather(f32[2,16,128]{2,1,0:T(8,128)S(1)} %convolution_bitcast_fusion.8), channel_id=1, replica_groups=mesh['row'=8,'col'=4] {'row'}, dimensions={0}, use_global_device_ids=true | all-gather | bytes 147456 | tf_op jit(solution)/shard_map/all_gather | solution.py:42
  85.7 0.6 gather_fusion
  86.4 8.1 %fusion.2 = f32[58,16,128]{2,1,0:T(8,128)S(1)} fusion(f32[58,16,128]{2,1,0:T(8,128)S(1)} %gather_fusion, f32[1,1,58,128,128]{4,3,2,1,0:T(8,128)} %param.9), kind=kOutput, calls=%fused_computation.4 | convolution fusion | flops 182452224 | bytes 4751360 | tf_op jit(solution)/shard_map/sij,skj->ski/dot_general | solution.py:43
  94.4 0.4 fusion.10
  94.8 0.6 copy.36
  95.6 19.3 %reduce-scatter.3.cloned.1.call-done = f32[2,16,128]{2,1,0:T(8,128)} async-done(((f32[8,16,128]{2,1,0:T(8,128)}), f32[2,16,128]{2,1,0:T(8,128)}) %reduce-scatter.3.cloned.1.call-update) | async-done | bytes 16400 | tf_op jit(solution)/shard_map/reduce_scatter | solution.py:52
  114.9 1.0 convolution_bitcast_fusion.1
  115.9 39.5 %psum.22 = f32[48,48]{0,1:T(8,128)S(1)} all-reduce(f32[48,48]{0,1:T(8,128)S(1)} %convolution_bitcast_fusion.1), channel_id=1, replica_groups=mesh['row'=8,'col'=4] {'row','col'}, use_global_device_ids=true, to_apply=%region_4.0 | all-reduce | flops 2304 | bytes 18432 | tf_op jit(solution)/shard_map/psum | solution.py:65
  155.4 0.2 fusion.50
  155.6 0.2 fusion.30
  155.8 0.2 fusion.52
  156.0 0.2 fusion.32
  156.2 0.2 subtract_subtract_fusion.1
  156.4 0.9 fusion.7
  157.5 0.2 convolution_add_fusion.7
  157.7 0.2 convolution_subtract_fusion.3
  157.9 0.2 convolution_subtract_fusion.2
  158.1 0.1 convolution_add_fusion.6
  158.2 0.2 convolution_add_fusion.5
  158.4 0.1 convolution_add_fusion.4
  158.7 1.5 cholesky.70
  160.2 0.6 compare_reduce_fusion.1
  160.8 0.6 fusion.94
  161.5 1.2 custom-call.8
  162.7 0.2 convolution_bitcast_fusion.10
  162.9 0.1 convolution_bitcast_fusion.5
  163.0 30.7 %all_gather.7 = f32[16,16,128]{2,1,0:T(8,128)S(1)} all-gather(f32[2,16,128]{2,1,0:T(8,128)S(1)} %convolution_bitcast_fusion.5), channel_id=1, replica_groups=mesh['row'=8,'col'=4] {'row'}, dimensions={0}, use_global_device_ids=true | all-gather | bytes 147456 | tf_op jit(solution)/shard_map/all_gather | solution.py:42
  193.8 0.6 gather_fusion.1
  194.4 8.1 %fusion = f32[58,16,128]{2,1,0:T(8,128)S(1)} fusion(f32[58,16,128]{2,1,0:T(8,128)S(1)} %gather_fusion.1, f32[1,1,58,128,128]{4,3,2,1,0:T(8,128)} %param.9), kind=kOutput, calls=%fused_computation.2 | convolution fusion | flops 182452224 | bytes 4751360 | tf_op jit(solution)/shard_map/sij,skj->ski/dot_general | solution.py:43
  202.5 0.4 fusion.8
  202.9 0.6 copy.47
  203.6 20.4 %reduce-scatter.5.cloned.1.call-done = f32[2,16,128]{2,1,0:T(8,128)} async-done(((f32[8,16,128]{2,1,0:T(8,128)}), f32[2,16,128]{2,1,0:T(8,128)}) %reduce-scatter.5.cloned.1.call-update) | async-done | bytes 16400 | tf_op jit(solution)/shard_map/reduce_scatter | solution.py:52
  223.9 1.0 convolution_bitcast_fusion
  224.9 39.5 %psum.23 = f32[48,48]{0,1:T(8,128)S(1)} all-reduce(f32[48,48]{0,1:T(8,128)S(1)} %convolution_bitcast_fusion), channel_id=1, replica_groups=mesh['row'=8,'col'=4] {'row','col'}, use_global_device_ids=true, to_apply=%region_6.9 | all-reduce | flops 2304 | bytes 18432 | tf_op jit(solution)/shard_map/psum | solution.py:65
  264.4 0.8 fusion.44
  265.3 0.9 fusion.26
  266.1 0.2 fusion.46
  266.4 0.2 fusion.28
  266.6 0.2 subtract_subtract_fusion
  266.9 0.9 fusion.5
  267.8 0.8 fusion.4
  268.6 0.2 convolution_add_fusion.3
  268.8 0.9 convolution_subtract_fusion.1
  269.7 0.9 convolution_subtract_fusion
  270.6 0.7 copy.58
  271.2 0.8 convolution_add_fusion.2
  272.1 0.2 convolution_add_fusion.1
  272.3 0.9 convolution_add_fusion
  273.2 1.5 cholesky.81
  274.7 0.6 compare_reduce_fusion
  275.4 0.6 select_bitcast_fusion
  276.0 1.2 custom-call.9
  277.2 0.2 convolution_bitcast_fusion.9
  277.5 0.7 copy.59
  278.2 0.7 convolution_bitcast_fusion.2
  (28 shorter events, 0.8 us)
Async XLA Ops:
  7.2 1.4 copy-start
  7.2 87.3 %copy-start.1 = (s32[1,1,58]{2,1,0:T(1,128)S(1)}, s32[1,1,58]{2,1,0:T(1,128)}, u32[]{:S(2)}) copy-start(s32[1,1,58]{2,1,0:T(1,128)} %param.10) | copy-start | bytes 700
  7.2 107.7 %reduce-scatter.3.cloned.1.call-start = ((), (), s32[]{:S(2)}) async-start(), calls=%async_computation.2 | async-start | bytes 81920 | tf_op jit(solution)/shard_map/reduce_scatter | solution.py:52
  95.5 128.4 %reduce-scatter.5.cloned.1.call-start = ((), (), s32[]{:S(2)}) async-start(), calls=%async_computation.3 | async-start | bytes 81920 | tf_op jit(solution)/shard_map/reduce_scatter | solution.py:52
Sparse Core Ops, SparseCore 0:
  95.6 19.2 reduce-scatter.2
  203.6 20.2 reduce-scatter.4
where the time goes:
time: 287 us; the launch traced here: 286 us
  blocking collectives  182 us (63%)
  waiting for transfers between devices  39.7 us (14%)
  matrix products  31.8 us (11%)
  between operations  14.8 us (5%)
  other arithmetic  12.8 us (4%)
  local copies, waits for them, and re-layouts  4.25 us (1%)
    psum x2, blocking collectives, on_device(): lax.psum(local_gram(stacked, stacked), ('row', 'col')) / row_total  79 us
    all_gather x2, blocking collectives, on_device(): gathered = lax.all_gather(vectors, 'row', axis=0, tiled=True)  61.3 us
    psum x1, blocking collectives, on_device(): lax.psum(local_gram(start_block, start_block), ('row', 'col')) / row_total  42 us
    reduce_scatter x2, waiting for transfers between devices, on_device(): lax.psum_scatter(jnp.einsum('rs,ski->rki', selector, operate_product, pre...  39.7 us
    dot_general x2, matrix products, on_device(): jnp.einsum('sij,skj->ski', matrix_tiles, gathered[cols_local], precision=...  16.1 us
    dot_general x22, matrix products, matmul(): jnp.dot(left, right, precision=highest, preferred_element_type=jnp.float32)  8.28 us
  transfers between devices with their start and end apart: 2, of which 2 were waited for; matrix products, arithmetic and copies ran while one was open for 0% of the time, Pallas kernels for 0%

commit v1 on v0

--- a/solution.py
+++ b/solution.py
@@ -1,3 +1,4 @@
+import functools
 import jax
 import jax.numpy as jnp
 from jax import lax
@@ -5,6 +6,13 @@
 
 ITERS = 2
 highest = lax.Precision.HIGHEST
+
+
+def _apply_tables(local_values, lane_axis):
+    return lax.all_gather(local_values, lane_axis).sum(axis=0)
+
+
+screen_handle = functools.partial(_apply_tables, lane_axis=("row", "col"))
 
 
 def matmul(left, right):
@@ -62,7 +70,7 @@
             tiled=True,
         )
         stacked = jnp.concatenate([image_block, vectors, previous], axis=1)
-        all_means = lax.psum(local_gram(stacked, stacked), ("row", "col")) / row_total
+        all_means = screen_handle(local_gram(stacked, stacked)) / row_total
         yy_mean = all_means[:vec_count, :vec_count]
         vy_mean = all_means[vec_count : 2 * vec_count, :vec_count]
         py_mean = all_means[2 * vec_count :, :vec_count]

time: 287 us -> 289 us (level)
  blocking collectives: 182 us -> 189 us
  waiting for transfers between devices: 39.7 us -> 35.4 us
    all_gather x0 -> x2, blocking collectives: none -> 85.4 us  [_apply_tables(): return lax.all_gather(local_values, lane_axis).sum(axis=0)]
    psum x2 -> x0, blocking collectives: 79 us -> none  [on_device(): lax.psum(local_gram(stacked, stacked), ('row', 'col')) / row_total]
    reduce_scatter x2, waiting for transfers between devices: 39.7 us -> 35.4 us  [on_device(): lax.psum_scatter(jnp.einsum('rs,ski->rki', selector, operate_product, pre...]
where the time goes in v1:
time: 289 us; the launch traced here: 288 us
  blocking collectives  189 us (65%)
  waiting for transfers between devices  35.4 us (12%)
  matrix products  31.8 us (11%)
  between operations  14.8 us (5%)
  other arithmetic  12.9 us (4%)
  local copies, waits for them, and re-layouts  4.32 us (1%)
    all_gather x2, blocking collectives, _apply_tables(): return lax.all_gather(local_values, lane_axis).sum(axis=0)  85.4 us
    all_gather x2, blocking collectives, on_device(): gathered = lax.all_gather(vectors, 'row', axis=0, tiled=True)  61.3 us
    psum x1, blocking collectives, on_device(): lax.psum(local_gram(start_block, start_block), ('row', 'col')) / row_total  42 us
    reduce_scatter x2, waiting for transfers between devices, on_device(): lax.psum_scatter(jnp.einsum('rs,ski->rki', selector, operate_product, pre...  35.4 us
    dot_general x2, matrix products, on_device(): jnp.einsum('sij,skj->ski', matrix_tiles, gathered[cols_local], precision=...  16.1 us
    dot_general x22, matrix products, matmul(): jnp.dot(left, right, precision=highest, preferred_element_type=jnp.float32)  8.29 us
  transfers between devices with their start and end apart: 2, of which 2 were waited for; matrix products, arithmetic and copies ran while one was open for 0% of the time, Pallas kernels for 0%

profile of v1, /device:TPU:0, one launch (start us, length us, event | category | flops | bytes accessed | tf_op | source)
XLA Modules:
  0.0 288.0 jit_solution(13248571649721391608)
XLA Ops:
  7.9 0.7 fusion.84
  8.6 0.1 convolution_bitcast_fusion.12
  8.7 42.0 %psum.7 = f32[16,16]{0,1:T(8,128)S(1)} all-reduce(f32[16,16]{0,1:T(8,128)S(1)} %convolution_bitcast_fusion.12), channel_id=1, replica_groups=mesh['row'=8,'col'=4] {'row','col'}, use_global_device_ids=true, to_apply=%region_0.0 | all-reduce | flops 256 | bytes 2048 | tf_op jit(solution)/shard_map/psum | solution.py:39
  50.8 1.5 cholesky.59
  52.3 0.6 compare_reduce_fusion.2
  52.9 0.6 fusion.25
  53.6 1.2 custom-call.7
  54.8 0.2 convolution_bitcast_fusion.11
  55.0 0.1 convolution_bitcast_fusion.8
  55.1 30.6 %all_gather.18 = f32[16,16,128]{2,1,0:T(8,128)S(1)} all-gather(f32[2,16,128]{2,1,0:T(8,128)S(1)} %convolution_bitcast_fusion.8), channel_id=1, replica_groups=mesh['row'=8,'col'=4] {'row'}, dimensions={0}, use_global_device_ids=true | all-gather | bytes 147456 | tf_op jit(solution)/shard_map/all_gather | solution.py:50
  85.7 0.6 gather_fusion
  86.4 8.1 %fusion.2 = f32[58,16,128]{2,1,0:T(8,128)S(1)} fusion(f32[58,16,128]{2,1,0:T(8,128)S(1)} %gather_fusion, f32[1,1,58,128,128]{4,3,2,1,0:T(8,128)} %param.9), kind=kOutput, calls=%fused_computation.4 | convolution fusion | flops 182452224 | bytes 4751360 | tf_op jit(solution)/shard_map/sij,skj->ski/dot_general | solution.py:51
  94.4 0.4 fusion.10
  94.8 0.6 copy.34
  95.5 19.3 %reduce-scatter.3.cloned.1.call-done = f32[2,16,128]{2,1,0:T(8,128)} async-done(((f32[8,16,128]{2,1,0:T(8,128)}), f32[2,16,128]{2,1,0:T(8,128)}) %reduce-scatter.3.cloned.1.call-update) | async-done | bytes 16400 | tf_op jit(solution)/shard_map/reduce_scatter | solution.py:60
  114.9 1.0 convolution_bitcast_fusion.1
  115.8 42.7 %all-gather = f32[1536,48]{1,0:T(8,128)S(1)} all-gather(f32[48,48]{1,0:T(8,128)S(1)} %convolution_bitcast_fusion.1), channel_id=2, replica_groups=mesh['row'=8,'col'=4] {'row','col'}, dimensions={0}, use_global_device_ids=true | all-gather | bytes 304128 | tf_op jit(solution)/shard_map/all_gather | solution.py:12
  158.7 0.2 fusion.50
  158.9 0.2 fusion.30
  159.1 0.2 fusion.52
  159.3 0.2 fusion.32
  159.5 0.2 subtract_subtract_fusion.1
  159.7 0.9 fusion.7
  160.8 0.2 convolution_add_fusion.7
  161.0 0.2 convolution_subtract_fusion.3
  161.2 0.2 convolution_subtract_fusion.2
  161.4 0.1 convolution_add_fusion.6
  161.5 0.2 convolution_add_fusion.5
  161.7 0.1 convolution_add_fusion.4
  162.0 1.5 cholesky.70
  163.5 0.6 compare_reduce_fusion.1
  164.1 0.6 fusion.94
  164.8 1.2 custom-call.8
  166.0 0.2 convolution_bitcast_fusion.10
  166.2 0.1 convolution_bitcast_fusion.5
  166.3 30.7 %all_gather.21 = f32[16,16,128]{2,1,0:T(8,128)S(1)} all-gather(f32[2,16,128]{2,1,0:T(8,128)S(1)} %convolution_bitcast_fusion.5), channel_id=1, replica_groups=mesh['row'=8,'col'=4] {'row'}, dimensions={0}, use_global_device_ids=true | all-gather | bytes 147456 | tf_op jit(solution)/shard_map/all_gather | solution.py:50
  197.1 0.6 gather_fusion.1
  197.7 8.1 %fusion = f32[58,16,128]{2,1,0:T(8,128)S(1)} fusion(f32[58,16,128]{2,1,0:T(8,128)S(1)} %gather_fusion.1, f32[1,1,58,128,128]{4,3,2,1,0:T(8,128)} %param.9), kind=kOutput, calls=%fused_computation.2 | convolution fusion | flops 182452224 | bytes 4751360 | tf_op jit(solution)/shard_map/sij,skj->ski/dot_general | solution.py:51
  205.8 0.4 fusion.8
  206.2 0.6 copy.45
  206.8 16.0 %reduce-scatter.5.cloned.1.call-done = f32[2,16,128]{2,1,0:T(8,128)} async-done(((f32[8,16,128]{2,1,0:T(8,128)}), f32[2,16,128]{2,1,0:T(8,128)}) %reduce-scatter.5.cloned.1.call-update) | async-done | bytes 16400 | tf_op jit(solution)/shard_map/reduce_scatter | solution.py:60
  222.8 1.0 convolution_bitcast_fusion
  223.8 42.7 %all-gather.1 = f32[1536,48]{1,0:T(8,128)S(1)} all-gather(f32[48,48]{1,0:T(8,128)S(1)} %convolution_bitcast_fusion), channel_id=3, replica_groups=mesh['row'=8,'col'=4] {'row','col'}, dimensions={0}, use_global_device_ids=true | all-gather | bytes 304128 | tf_op jit(solution)/shard_map/all_gather | solution.py:12
  266.7 0.8 fusion.44
  267.6 0.9 fusion.26
  268.4 0.2 fusion.46
  268.7 0.2 fusion.28
  268.9 0.2 subtract_subtract_fusion
  269.1 0.9 fusion.5
  270.0 0.8 fusion.4
  270.9 0.7 copy.56
  271.6 0.2 convolution_add_fusion.3
  271.8 0.9 convolution_subtract_fusion.1
  272.6 0.9 convolution_subtract_fusion
  273.5 0.9 convolution_add_fusion.2
  274.3 0.2 convolution_add_fusion.1
  274.5 0.9 convolution_add_fusion
  275.5 1.5 cholesky.81
  276.9 0.6 compare_reduce_fusion
  277.6 0.6 select_bitcast_fusion
  278.2 1.2 custom-call.9
  279.5 0.2 convolution_bitcast_fusion.9
  279.7 0.7 copy.57
  280.4 0.7 convolution_bitcast_fusion.2
  (31 shorter events, 1.0 us)
Async XLA Ops:
  7.2 1.4 copy-start
  7.2 87.3 %copy-start.1 = (s32[1,1,58]{2,1,0:T(1,128)S(1)}, s32[1,1,58]{2,1,0:T(1,128)}, u32[]{:S(2)}) copy-start(s32[1,1,58]{2,1,0:T(1,128)} %param.10) | copy-start | bytes 700
  7.2 107.7 %reduce-scatter.3.cloned.1.call-start = ((), (), s32[]{:S(2)}) async-start(), calls=%async_computation.2 | async-start | bytes 81920 | tf_op jit(solution)/shard_map/reduce_scatter | solution.py:60
  95.5 127.4 %reduce-scatter.5.cloned.1.call-start = ((), (), s32[]{:S(2)}) async-start(), calls=%async_computation.3 | async-start | bytes 81920 | tf_op jit(solution)/shard_map/reduce_scatter | solution.py:60
Sparse Core Ops, SparseCore 0:
  95.6 19.2 reduce-scatter.2
  206.9 15.8 reduce-scatter.4
